TPU v7x, 32 devices: a whole 2x2x4 slice. The times are simulated.
32 devices in a mesh: chan: 8 (over z, y), facet: 4 (over x, core).
Axes of the slice: x: 2, y: 2, z: 4, core: 2. Of those that a mesh axis runs over, the one named last changes fastest.
Arguments:
- solution: float32 [8, 2048, 2048], P('chan', 'facet'), may hold values from -6 to 6
- residual: float32 [8, 2048, 2048], P('chan', 'facet'), may hold values from -120 to 120
- direction: float32 [8, 2048, 2048], P('chan', 'facet'), may hold values from -120 to 120
- spectra: float32 [8, 4096, 4096], P('chan', None, 'facet'), may hold values from 0.05 to 1
- basis: float32 [8, 8], replicated, may hold values from -2 to 2
- slot_channel: int32 [8], replicated, may hold values from 0 to 7, each once
Outputs:
- new_solution: float32 [8, 2048, 2048], P('chan', 'facet')
- new_residual: float32 [8, 2048, 2048], P('chan', 'facet')
- new_direction: float32 [8, 2048, 2048], P('chan', 'facet')
Inputs may be any that keep to these rules, and one draw needn't show every extreme that they name: `slot_channel`: every channel appears in exactly one slot.
All inputs are finite; a program needn't handle non-finite values.
Results may differ from a plain program's by a relative error of at most 0.000064.
Values sent between devices are 32-bit elements; how exact they have to be, the bound alone decides.
A program may use at most 256 MiB of HBM per device.

v0:
```python
import math
import jax
import jax.numpy as jnp
from jax import lax
from jax.sharding import PartitionSpec as P

ROOT = 64
HIGH = lax.Precision.HIGH
HIGHEST = lax.Precision.HIGHEST
PRIOR_FLOOR = 0.25


def wave(product, length, direction_sign):
    angles = (product % length).astype(jnp.float32) * (2.0 * math.pi / length)
    return (jnp.cos(angles), direction_sign * jnp.sin(angles))


def span(size):
    return jnp.arange(size, dtype=jnp.int32)


def swap_pairs(array, count, bit):
    pairs = [(place, place ^ bit) for place in range(count)]
    return lax.ppermute(array, "facet", pairs)


def column_table(width, columns, length, first_column):
    column = first_column + span(columns)[None, :]
    coarse = width // ROOT
    coarse_real, coarse_imag = wave(span(coarse)[:, None] * ROOT * column, length, -1.0)
    fine_real, fine_imag = wave(span(ROOT)[:, None] * column, length, -1.0)
    coarse_real, coarse_imag = (coarse_real[:, None], coarse_imag[:, None])
    fine_real, fine_imag = (fine_real[None], fine_imag[None])
    table_real = (coarse_real * fine_real - coarse_imag * fine_imag).reshape(width, columns)
    table_imag = (coarse_real * fine_imag + coarse_imag * fine_real).reshape(width, columns)
    return lax.optimization_barrier((table_real, table_imag))


def complex_stack(real, imag):
    return jnp.stack([jnp.stack([real, imag]), jnp.stack([-imag, real])])


def row_spectrum_pass(planes, spectrum, row_digits, factor):
    halved, columns = (row_digits.shape[0], planes.shape[2])
    blocks = planes.reshape(2, halved, factor, columns)
    first = complex_stack(*wave(row_digits[:, None] * span(factor)[None, :], factor, -1.0))
    section = jnp.einsum("pjnc,pqjk->kqnc", blocks, first, precision=HIGH)
    spread = (
        span(factor)[:, None, None] * span(factor)[None, :, None]
        + span(factor)[None, :, None] * span(factor)[None, None, :] * factor
    )
    second = complex_stack(*wave(spread, factor * factor, -1.0))
    freqs = jnp.einsum("kpnc,pqknj->kqjc", section, second, precision=HIGH)
    spectrum = spectrum.reshape(factor, factor, columns).transpose(1, 0, 2)
    weighted = freqs * spectrum[:, None]
    third = complex_stack(*wave(spread, factor * factor, 1.0))
    section = jnp.einsum("kpjc,pqknj->kqnc", weighted, third, precision=HIGH)
    last = complex_stack(*wave(row_digits[:, None] * span(factor)[None, :], factor, 1.0))
    rows = jnp.einsum("kpnc,pqjk->qjnc", section, last, precision=HIGH)
    return rows.reshape(2, halved * factor, columns)


def body(solution, residual, direction, spectra, basis, slot_channel):
    channel_count = basis.shape[0]
    factor = ROOT
    length = factor * factor
    facets = lax.axis_size("facet")
    place = lax.axis_index("facet")
    height, width = direction.shape[1:]
    columns = spectra.shape[2]
    own = direction[0]
    blocks = {0: own}
    bit = facets // 2
    while bit:
        blocks.update({key ^ bit: swap_pairs(blocks[key], facets, bit) for key in list(blocks)})
        bit //= 2
    table_real, table_imag = column_table(width, columns, length, place * columns)
    near = [blocks[key] for key in range(facets // 2)]
    far = [blocks[key] for key in range(facets // 2, facets)]
    near_rows = jnp.concatenate(near, axis=0)
    far_rows = jnp.concatenate(far, axis=0)
    planes = jnp.stack(
        [
            jnp.concatenate(
                [jnp.dot(part, table, precision=HIGH) for part in (near_rows, far_rows)], axis=0
            )
            for table in (table_real, table_imag)
        ]
    )
    digits = height // factor
    row_digits = ((place ^ span(facets))[:, None] * digits + span(digits)[None, :]).reshape(-1)
    rows = row_spectrum_pass(planes, spectra[0], row_digits, factor)

    def partial(part):
        wide = (((1,), (1,)), ((), ()))
        return lax.dot_general(part[0], table_real, wide, precision=HIGH) + lax.dot_general(
            part[1], table_imag, wide, precision=HIGH
        )

    sums = {}
    half = facets // 2
    for base in (half, 0):
        image = partial(rows[:, base * height : (base + half) * height])
        for key in range(half):
            sums[base + key] = image[key * height : (key + 1) * height]
    bit = 1
    while bit < facets:
        sums = {
            key: sums[key] + swap_pairs(sums[key | bit], facets, bit)
            for key in sorted(sums, reverse=True)
            if not key & bit
        }
        bit *= 2
    blurred = sums[0][None] * (1.0 / float(length * length))
    regrouped = lax.all_to_all(direction, "chan", split_axis=1, concat_axis=0, tiled=True)
    one_hot = (slot_channel[:, None] == span(channel_count)[None, :]).astype(jnp.float32)
    loadings = jnp.dot(one_hot, basis, precision=HIGHEST)
    coeffs = jnp.einsum("cq,cij->qij", loadings, regrouped, precision=HIGHEST)
    local_prior = PRIOR_FLOOR * regrouped + jnp.einsum(
        "cq,qij->cij", loadings, coeffs, precision=HIGHEST
    )
    prior_term = lax.all_to_all(local_prior, "chan", split_axis=0, concat_axis=1, tiled=True)
    applied = blurred + prior_term
    moments = jnp.stack(
        [
            jnp.sum(residual * residual),
            jnp.sum(direction * applied),
            jnp.sum(residual * applied),
            jnp.sum(applied * applied),
        ]
    )
    norm_now, curvature, cross, square = lax.psum(moments, ("chan", "facet"))
    step_size = norm_now / curvature
    new_solution = solution + step_size * direction
    new_residual = residual - step_size * applied
    norm_next = norm_now - 2.0 * step_size * cross + step_size * step_size * square
    new_direction = new_residual + norm_next / norm_now * direction
    return (new_solution, new_residual, new_direction)


def solution(mesh):
    return jax.shard_map(
        body,
        mesh=mesh,
        in_specs=(
            P("chan", "facet", None),
            P("chan", "facet", None),
            P("chan", "facet", None),
            P("chan", None, "facet"),
            P(),
            P(),
        ),
        out_specs=(P("chan", "facet", None), P("chan", "facet", None), P("chan", "facet", None)),
        check_vma=False,
    )
```

profile of v0, /device:TPU:0, one launch (start us, length us, event | category | flops | bytes accessed | tf_op | source)
XLA Modules:
  0.0 682.2 jit_solution(11598784250257221795)
XLA Ops:
  0.6 3.0 collective-permute-start.1
  3.7 8.5 %copy.27 = f32[1,512,2048]{2,0,1:T(1,128)} copy(f32[1,512,2048]{2,1,0:T(8,128)} %param.8) | data formatting | bytes 8388608 | tf_op args[2]
  12.2 6.1 all-to-all-start
  19.2 1.0 fusion.54
  20.3 7.1 %multiply_add_fusion = (f32[32,64,1024]{2,1,0:T(8,128)}, f32[32,64,1024]{2,1,0:T(8,128)}) fusion(f32[64,1024]{1,0:T(8,128)S(1)} %get-tuple-element.32, f32[32,1024]{1,0:T(8,128)S(1)} %get-tuple-element.30, f32[64,1024]{1,0:T(8,128)S(1)} %get-tuple-element.31, f32[32,1024]{1,0:T(8,128)S(1)} %get-tuple-element.29), kind=kLoop, calls=%fused_computation.23 | loop fusion | flops 12582912 | bytes 17563648 | tf_op jit(solution)/shard_map/add | solution.py:35
  27.4 67.2 %collective-permute-done.1 = f32[512,2048]{1,0:T(8,128)} collective-permute-done((f32[512,2048]{1,0:T(8,128)}, f32[512,2048]{1,0:T(8,128)}, u32[]{:S(2)}, u32[]{:S(2)}) %collective-permute-start.1) | collective-permute-done | bytes 4194336 | tf_op jit(solution)/shard_map/ppermute | solution.py:24
  94.7 17.8 %copy.73 = f32[64,64,1024]{2,0,1:T(8,128)} copy(f32[64,64,1024]{2,1,0:T(8,128)} %bitcast.135) | data formatting | bytes 33554432 | tf_op jit(solution)/shard_map/reshape;squeeze | solution.py:54
  112.4 9.1 %fusion.41 = (f32[1,64,64,64]{2,3,1,0:T(8,128)S(1)}, f32[1,64,64,64]{2,3,1,0:T(8,128)S(1)}, f32[1,64,64,64]{2,3,1,0:T(8,128)S(1)}, f32[1,64,64,64]{2,3,1,0:T(8,128)S(1)}, f32[1,64,64,64]{2,3,1,0:T(8,128)}) fusion(s32[64,64]{0,1:T(8,128)S(1)} %broadcast_multiply_fusion.1, s32[64,64]{1,0:T(8,128)S(1)} %copy.17), kind=kLoop, calls=%fused_computation.73 | loop fusion | flops 4456448 | bytes 5275648 | tf_op jit(solution)/shard_map/sin | solution.py:15
  121.6 4.8 fusion.23
  126.3 6.8 pad_maximum_fusion
  133.1 5.0 constant_dynamic-update-slice_fusion.1
  138.1 18.5 %fusion.17 = f32[1024,1024]{1,0:T(8,128)} fusion(f32[2048,1024]{1,0:T(8,128)} %bitcast.142, f32[512,2048]{1,0:T(8,128)} %collective-permute-done, f32[512,2048]{1,0:T(8,128)S(1)} %bitcast.129), kind=kOutput, calls=%fused_computation.26 | convolution fusion | flops 12886999040 | bytes 20971520 | tf_op jit(solution)/shard_map/dot_general | solution.py:85
  156.6 14.4 %fusion.16 = f32[1024,1024]{1,0:T(8,128)S(1)} fusion(f32[2048,1024]{1,0:T(8,128)S(1)} %bitcast.152, f32[512,2048]{1,0:T(8,128)} %collective-permute-done, f32[512,2048]{1,0:T(8,128)S(1)} %bitcast.130), kind=kOutput, calls=%fused_computation.25 | convolution fusion | flops 12886999040 | bytes 20971520 | tf_op jit(solution)/shard_map/dot_general | solution.py:85
  171.1 4.7 constant_dynamic-update-slice_fusion
  175.7 17.8 %fusion.79 = f32[1024,1024]{1,0:T(8,128)} fusion(f32[1024,2048]{1,0:T(8,128)} %constant_dynamic-update-slice_fusion, f32[2048,1024]{1,0:T(8,128)S(1)} %bitcast.147), kind=kOutput, calls=%fused_computation.140 | convolution fusion | flops 12884901888 | bytes 20971520 | tf_op jit(solution)/shard_map/dot_general | solution.py:85
  193.6 17.6 %fusion.80 = f32[1024,1024]{1,0:T(8,128)} fusion(f32[1024,2048]{1,0:T(8,128)} %constant_dynamic-update-slice_fusion, f32[2048,1024]{1,0:T(8,128)S(1)} %bitcast.153), kind=kOutput, calls=%fused_computation.141 | convolution fusion | flops 12884901888 | bytes 20971520 | tf_op jit(solution)/shard_map/dot_general | solution.py:85
  211.2 4.3 pad_maximum_fusion.3
  215.5 8.1 %copy.19 = f32[1,32,64,1024]{3,1,0,2:T(8,128)} copy(f32[1,32,64,1024]{3,2,1,0:T(8,128)S(1)} %bitcast.133) | data formatting | bytes 16777216 | tf_op jit(solution)/shard_map/stack | solution.py:82
  223.6 3.3 pad_maximum_fusion.4
  226.9 8.1 %copy.20 = f32[1,32,64,1024]{3,1,0,2:T(8,128)} copy(f32[1,32,64,1024]{3,2,1,0:T(8,128)S(1)} %bitcast.134) | data formatting | bytes 16777216 | tf_op jit(solution)/shard_map/stack | solution.py:82
  235.4 27.6 %convolution_bitcast_fusion = f32[64,2,64,1024,1]{3,0,2,1,4:T(8,128)} fusion(f32[1,32,64,1024]{3,1,0,2:T(8,128)} %copy.20, f32[1,32,64,1024]{3,1,0,2:T(8,128)} %copy.19, f32[1,2,32,64]{3,2,0,1:T(8,128)S(1)} %get-tuple-element.26, f32[1,2,32,64]{3,2,0,1:T(8,128)S(1)} %get-tuple-element.27), kind=kOutput, calls=%fused_computation.9 | convolution fusion | flops 3225427968 | bytes 50364416 | tf_op jit(solution)/shard_map/pjnc,pqjk->kqnc/dot_general | solution.py:47
  263.0 47.3 %fusion.4 = f32[64,2,64,1024,1]{3,2,1,0,4:T(8,128)} fusion(f32[64,2,64,1024,1]{3,0,2,1,4:T(8,128)} %convolution_bitcast_fusion, f32[2,2,64,64,64]{3,4,2,1,0:T(8,128)} %get-tuple-element.43), kind=kOutput, calls=%fused_computation.5 | convolution fusion | flops 6442450944 | bytes 71303168 | tf_op jit(solution)/shard_map/kpnc,pqknj->kqjc/dot_general | solution.py:53
  310.3 31.7 %fusion.11 = f32[64,2,64,1024]{3,2,1,0:T(8,128)} fusion(f32[64,2,64,1024,1]{3,2,1,0,4:T(8,128)} %fusion.4, f32[64,64,1024]{2,1,0:T(8,128)} %bitcast.126, f32[2,2,64,64,64]{3,4,2,1,0:T(8,128)} %get-tuple-element.42), kind=kOutput, calls=%fused_computation.15 | convolution fusion | flops 6450839552 | bytes 88080384 | tf_op jit(solution)/shard_map/kpjc,pqknj->kqnc/dot_general | solution.py:57
  342.0 40.1 %fusion.18 = f32[2,32,64,1024]{3,1,2,0:T(8,128)S(1)} fusion(f32[64,2,64,1024]{3,2,1,0:T(8,128)} %fusion.11, f32[1,2,32,64]{3,2,1,0:T(8,128)S(1)} %get-tuple-element.28, f32[1,2,32,64]{3,2,1,0:T(8,128)S(1)} %get-tuple-element.25), kind=kOutput, calls=%fused_computation.27 | convolution fusion | flops 3221233664 | bytes 50364416 | tf_op jit(solution)/shard_map/kpnc,pqjk->qjnc/dot_general | solution.py:59
  382.2 19.4 %copy.26 = f32[2,32,64,1024]{3,2,1,0:T(8,128)} copy(f32[2,32,64,1024]{3,1,2,0:T(8,128)S(1)} %fusion.18) | data formatting | bytes 33554432 | tf_op jit(solution)/shard_map/kpnc,pqjk->qjnc/dot_general | solution.py:59
  401.6 16.8 %fusion.25 = f32[1024,2048]{1,0:T(8,128)S(1)} fusion(f32[2048,1024]{1,0:T(8,128)} %bitcast.148, f32[2,2048,1024]{2,1,0:T(8,128)} %bitcast.136), kind=kOutput, calls=%fused_computation.38 | convolution fusion | flops 12884901888 | bytes 20971520 | tf_op jit(solution)/shard_map/dot_general | solution.py:96
  418.4 18.0 %fusion.37 = f32[1024,2048]{1,0:T(8,128)S(1)} fusion(f32[1024,2048]{1,0:T(8,128)S(1)} %fusion.25, f32[2048,1024]{1,0:T(8,128)} %bitcast.143, f32[2,2048,1024]{2,1,0:T(8,128)} %bitcast.137), kind=kOutput, calls=%fused_computation.65 | convolution fusion | flops 12886999040 | bytes 29360128 | tf_op jit(solution)/shard_map/dot_general | solution.py:96
  436.4 2.5 slice.45
  438.9 2.0 copy-done.3
  441.6 4.2 copy.48
  445.7 6.0 fusion.34
  451.8 6.6 multiply_add_fusion.3
  458.3 4.4 copy.31
  462.8 6.1 all-to-all-start.1
  468.8 18.3 %fusion.30 = f32[1024,2048]{1,0:T(8,128)} fusion(f32[2048,1024]{1,0:T(8,128)} %bitcast.149, f32[2,2048,1024]{2,1,0:T(8,128)} %bitcast.138), kind=kOutput, calls=%fused_computation.46 | convolution fusion | flops 12884901888 | bytes 20971520 | tf_op jit(solution)/shard_map/dot_general | solution.py:96
  487.2 18.1 %fusion.36 = f32[1024,2048]{1,0:T(8,128)S(1)} fusion(f32[1024,2048]{1,0:T(8,128)} %fusion.30, f32[2048,1024]{1,0:T(8,128)} %bitcast.144, f32[2,2048,1024]{2,1,0:T(8,128)} %bitcast.139), kind=kOutput, calls=%fused_computation.64 | convolution fusion | flops 12886999040 | bytes 29360128 | tf_op jit(solution)/shard_map/dot_general | solution.py:96
  505.5 3.0 copy-done.4
  508.5 5.0 slice_add_fusion
  513.6 1.5 collective-permute-start.5
  515.0 0.7 collective-permute-done.3
  515.8 46.5 %all-to-all-done.1 = f32[8,64,2048]{2,1,0:T(8,128)} async-done(((f32[8,64,2048]{2,1,0:T(8,128)}), f32[8,64,2048]{2,1,0:T(8,128)}, u32[]{:S(2)}, u32[]{:S(2)}) %all-to-all-start.1) | async-done | bytes 4194336 | tf_op jit(solution)/shard_map/all_to_all | solution.py:122
  562.3 44.5 %collective-permute-done.5 = f32[512,2048]{1,0:T(8,128)} collective-permute-done((f32[512,2048]{1,0:T(8,128)}, f32[512,2048]{1,0:T(8,128)}, u32[]{:S(2)}, u32[]{:S(2)}) %collective-permute-start.5) | collective-permute-done | bytes 4194336 | tf_op jit(solution)/shard_map/ppermute | solution.py:24
  606.8 10.3 %multiply_reduce_fusion.1 = (f32[]{:T(128)}, f32[]{:T(128)}, f32[]{:T(128)}, f32[512,2048]{1,0:T(8,128)S(1)}) fusion(f32[1,512,2048]{2,1,0:T(8,128)} %param.7, f32[1,512,2048]{2,1,0:T(8,128)} %param.8, f32[8,64,2048]{2,1,0:T(8,128)} %all-to-all-done.1, f32[512,2048]{1,0:T(8,128)} %collective-permute-done.5, f32[512,2048]{1,0:T(8,128)} %collective-permute-done.3, ...), kind=kLoop, calls=%fused_computation.58 | loop fusion | flops 10485757 | bytes 29360140 | tf_op jit(solution)/shard_map/reduce_sum | solution.py:126
  617.2 2.0 copy-done.2
  619.2 1.7 multiply_reduce_fusion
  620.9 2.6 pad_maximum_fusion.15
  623.5 40.9 %psum.7 = f32[4]{0:T(128)S(1)} all-reduce(f32[4]{0:T(128)S(1)} %pad_maximum_fusion.15), channel_id=1, replica_groups=mesh['chan'=8,'facet'=4] {'chan','facet'}, use_global_device_ids=true, to_apply=%region_4.5 | all-reduce | flops 4 | bytes 32 | tf_op jit(solution)/shard_map/psum | solution.py:132
  669.1 12.8 %multiply_add_fusion.1 = (f32[1,512,2048]{2,1,0:T(8,128)}, f32[1,512,2048]{2,1,0:T(8,128)}, f32[1,512,2048]{2,1,0:T(8,128)}) fusion(f32[1,512,2048]{2,1,0:T(8,128)} %param.8, f32[]{:T(128)S(6)} %div.7, f32[1,512,2048]{2,1,0:T(8,128)} %param.7, f32[512,2048]{1,0:T(8,128)} %copy-done.2, f32[]{:T(128)S(6)} %div.6, f32[1,512,2048]{2,1,0:T(8,128)} %param.6), kind=kLoop, calls=%fused_computation.54 | loop fusion | flops 6291456 | bytes 29360136 | tf_op jit(solution)/shard_map/add | solution.py:137
  (46 shorter events, 2.6 us)
Async XLA Ops:
  0.6 440.7 %copy-start = (f32[8,8]{1,0:T(8,128)S(1)}, f32[8,8]{1,0:T(8,128)}, u32[]{:S(2)}) copy-start(f32[8,8]{1,0:T(8,128)} %param.10) | copy-start | bytes 772
  0.6 93.9 %collective-permute-start.1 = (f32[512,2048]{1,0:T(8,128)}, f32[512,2048]{1,0:T(8,128)}, u32[]{:S(2)}, u32[]{:S(2)}) collective-permute-start(f32[512,2048]{1,0:T(8,128)} %bitcast.127), channel_id=1, source_target_pairs={{0,2},{1,3},{2,0},{3,1},{4,6},{5,7},{6,4},{7,5},{8,10},{9,11},{10,... | collective-permute-start | bytes 12582920 | tf_op jit(solution)/shard_map/ppermute | solution.py:24
  3.7 134.4 %collective-permute-start = (f32[512,2048]{1,0:T(8,128)}, f32[512,2048]{1,0:T(8,128)}, u32[]{:S(2)}, u32[]{:S(2)}) collective-permute-start(f32[512,2048]{1,0:T(8,128)} %bitcast.128), channel_id=1, source_target_pairs={{0,1},{1,0},{2,3},{3,2},{4,5},{5,4},{6,7},{7,6},{8,9},{9,8},{10,11... | collective-permute-start | bytes 12582920 | tf_op jit(solution)/shard_map/ppermute | solution.py:24
  12.2 429.3 %all-to-all-start = ((f32[1,512,2048]{2,0,1:T(1,128)}), f32[1,512,2048]{2,0,1:T(1,128)}, u32[]{:S(2)}, u32[]{:S(2)}) async-start(f32[1,512,2048]{2,0,1:T(1,128)} %copy.27), calls=%async_computation | async-start | bytes 8388608 | tf_op jit(solution)/shard_map/all_to_all | solution.py:115
  94.6 76.5 %collective-permute-start.2 = (f32[512,2048]{1,0:T(8,128)}, f32[512,2048]{1,0:T(8,128)}, u32[]{:S(2)}, u32[]{:S(2)}) collective-permute-start(f32[512,2048]{1,0:T(8,128)} %collective-permute-done.1), channel_id=1, source_target_pairs={{0,1},{1,0},{2,3},{3,2},{4,5},{5,4},{6,7},{7,6},{8,9},{9,8},{10,11... | collective-permute-start | bytes 12582920 | tf_op jit(solution)/shard_map/ppermute | solution.py:24
  133.1 5.0 copy-start.1
  133.1 23.5 %slice-start.4 = ((s8[8388608]{0:T(1024)(128)(4,1)}), s8[4194304]{0:T(1024)(128)(4,1)S(1)}, s32[]{:S(2)}) async-start(s8[8388608]{0:T(1024)(128)(4,1)} %bitcast.150), calls=%async_computation.6 | async-start | bytes 8388608
  138.1 18.5 %slice-start.5 = ((s8[8388608]{0:T(1024)(128)(4,1)}), s8[4194304]{0:T(1024)(128)(4,1)S(1)}, s32[]{:S(2)}) async-start(s8[8388608]{0:T(1024)(128)(4,1)} %bitcast.150), calls=%async_computation.7 | async-start | bytes 8388608
  138.1 37.7 %slice-start.2 = ((s8[8388608]{0:T(1024)(128)(4,1)}), s8[4194304]{0:T(1024)(128)(4,1)S(1)}, s32[]{:S(2)}) async-start(s8[8388608]{0:T(1024)(128)(4,1)} %bitcast.145), calls=%async_computation.4 | async-start | bytes 8388608
  156.6 19.1 %slice-start.3 = ((s8[8388608]{0:T(1024)(128)(4,1)}), s8[4194304]{0:T(1024)(128)(4,1)S(1)}, s32[]{:S(2)}) async-start(s8[8388608]{0:T(1024)(128)(4,1)} %bitcast.145), calls=%async_computation.5 | async-start | bytes 8388608
  436.4 4.5 copy-start.3
  436.4 5.0 copy-start.5
  440.9 67.6 %collective-permute-start.4 = (f32[512,2048]{1,0:T(8,128)}, f32[512,2048]{1,0:T(8,128)}, u32[]{:S(2)}, u32[]{:S(2)}) collective-permute-start(f32[512,2048]{1,0:T(8,128)} %slice.45), channel_id=1, source_target_pairs={{0,1},{1,0},{2,3},{3,2},{4,5},{5,4},{6,7},{7,6},{8,9},{9,8},{10,11... | collective-permute-start | bytes 12582920 | tf_op jit(solution)/shard_map/ppermute | solution.py:24
  462.8 99.5 %all-to-all-start.1 = ((f32[8,64,2048]{2,1,0:T(8,128)}), f32[8,64,2048]{2,1,0:T(8,128)}, u32[]{:S(2)}, u32[]{:S(2)}) async-start(f32[8,64,2048]{2,1,0:T(8,128)} %copy.31), calls=%async_computation.1 | async-start | bytes 8388608 | tf_op jit(solution)/shard_map/all_to_all | solution.py:122
  468.8 39.7 %slice-start = ((s8[8388608]{0:T(1024)(128)(4,1)}), s8[4194304]{0:T(1024)(128)(4,1)S(1)}, s32[]{:S(2)}) async-start(s8[8388608]{0:T(1024)(128)(4,1)} %bitcast.140), calls=%async_computation.2 | async-start | bytes 8388608
  487.2 21.3 %slice-start.1 = ((s8[8388608]{0:T(1024)(128)(4,1)}), s8[4194304]{0:T(1024)(128)(4,1)S(1)}, s32[]{:S(2)}) async-start(s8[8388608]{0:T(1024)(128)(4,1)} %bitcast.140), calls=%async_computation.3 | async-start | bytes 8388608
  505.2 3.2 copy-start.4
  508.5 7.3 %collective-permute-start.3 = (f32[512,2048]{1,0:T(8,128)S(1)}, f32[512,2048]{1,0:T(8,128)}, u32[]{:S(2)}, u32[]{:S(2)}) collective-permute-start(f32[512,2048]{1,0:T(8,128)S(1)} %slice.41), channel_id=1, source_target_pairs={{0,1},{1,0},{2,3},{3,2},{4,5},{5,4},{6,7},{7,6},{8,9},{9,8},{10,11... | collective-permute-start | bytes 12582920 | tf_op jit(solution)/shard_map/ppermute | solution.py:24
  513.6 93.3 %collective-permute-start.5 = (f32[512,2048]{1,0:T(8,128)}, f32[512,2048]{1,0:T(8,128)}, u32[]{:S(2)}, u32[]{:S(2)}) collective-permute-start(f32[512,2048]{1,0:T(8,128)} %slice_add_fusion), channel_id=1, source_target_pairs={{0,2},{1,3},{2,0},{3,1},{4,6},{5,7},{6,4},{7,5},{8,10},{9,11},{10,... | collective-permute-start | bytes 12582920 | tf_op jit(solution)/shard_map/ppermute | solution.py:24
  617.2 2.0 copy-start.2
where the time goes:
time: 687 us; the launch traced here: 682 us
  matrix products  299 us (44%)
  waiting for transfers between devices  159 us (23%)
  local copies, waits for them, and re-layouts  90.7 us (13%)
  other arithmetic  69.8 us (10%)
  blocking collectives  40.9 us (6%)
  starting transfers between devices  17.2 us (3%)
    ppermute x6, waiting for transfers between devices, swap_pairs(): return lax.ppermute(array, 'facet', pairs)  112 us
    dot_general x4, matrix products, body(): jnp.dot(part, table, precision=HIGH)  68.4 us
    dot_general x1, matrix products, row_spectrum_pass(): freqs = jnp.einsum('kpnc,pqknj->kqjc', section, second, precision=HIGH)  47.3 us
    all_to_all x1, waiting for transfers between devices, body(): lax.all_to_all(local_prior, 'chan', split_axis=0, concat_axis=1, tiled=True)  46.5 us
    psum x1, blocking collectives, body(): norm_now, curvature, cross, square = lax.psum(moments, ('chan', 'facet'))  40.9 us
    dot_general x1, matrix products, row_spectrum_pass(): rows = jnp.einsum('kpnc,pqjk->qjnc', section, last, precision=HIGH)  40.1 us
    dot_general x2, matrix products, partial(): lax.dot_general(part[0], table_real, wide, precision=HIGH)  36 us
    dot_general x2, matrix products, partial(): lax.dot_general(part[1], table_imag, wide, precision=HIGH)  35.1 us
  transfers between devices with their start and end apart: 8, of which 4 were waited for; matrix products, arithmetic and copies ran while one was open for 62% of the time, Pallas kernels for 0%

commit v1 on v0

--- a/solution.py
+++ b/solution.py
@@ -119,7 +119,15 @@
     local_prior = PRIOR_FLOOR * regrouped + jnp.einsum(
         "cq,qij->cij", loadings, coeffs, precision=HIGHEST
     )
-    prior_term = lax.all_to_all(local_prior, "chan", split_axis=0, concat_axis=1, tiled=True)
+    ways, here = (lax.axis_size("chan"), lax.axis_index("chan"))
+    width_2 = local_prior.shape[0] // ways
+    turned = jnp.roll(local_prior, -here * width_2, axis=0)
+    got = [lax.slice_in_dim(turned, 0, width_2, axis=0)]
+    for hop in range(1, ways):
+        sent = lax.slice_in_dim(turned, hop * width_2, (hop + 1) * width_2, axis=0)
+        got.append(lax.ppermute(sent, "chan", [(d, (d + hop) % ways) for d in range(ways)]))
+    line = jnp.concatenate(got[::-1], axis=1)
+    prior_term = jnp.roll(line, (here + 1) * got[0].shape[1], axis=1)
     applied = blurred + prior_term
     moments = jnp.stack(
         [

time: 687 us -> 657 us (0.956)
  waiting for transfers between devices: 159 us -> 123 us
  other arithmetic: 69.8 us -> 61.1 us
  starting transfers between devices: 17.2 us -> 25.1 us
  matrix products: 299 us -> 306 us
    ppermute x0 -> x7, waiting for transfers between devices: none -> 47.9 us  [body(): lax.ppermute(sent, 'chan', [(d, (d + hop) % ways) for d in range(ways)])]
    all_to_all x1 -> x0, waiting for transfers between devices: 46.5 us -> none  [body(): lax.all_to_all(local_prior, 'chan', split_axis=0, concat_axis=1, tiled=True)]
    ppermute x6, waiting for transfers between devices: 112 us -> 74.8 us  [swap_pairs(): return lax.ppermute(array, 'facet', pairs)]
    ppermute x0 -> x7, starting transfers between devices: none -> 13.8 us  [body(): lax.ppermute(sent, 'chan', [(d, (d + hop) % ways) for d in range(ways)])]
    unnamed x27 -> x68, local copies, waits for them, and re-layouts: 24.7 us -> 25.6 us
  transfers between devices with their start and end apart: 8 -> 14, of which waited for: 4 -> 4; matrix products, arithmetic and copies ran while one was open for 62% -> 25% of each run, Pallas kernels for 0% -> 0%
where the time goes in v1:
time: 657 us; the launch traced here: 652 us
  matrix products  306 us (47%)
  waiting for transfers between devices  123 us (19%)
  local copies, waits for them, and re-layouts  93.5 us (14%)
  other arithmetic  61.1 us (9%)
  blocking collectives  38.2 us (6%)
  starting transfers between devices  25.1 us (4%)
    ppermute x6, waiting for transfers between devices, swap_pairs(): return lax.ppermute(array, 'facet', pairs)  74.8 us
    dot_general x4, matrix products, body(): jnp.dot(part, table, precision=HIGH)  72 us
    ppermute x7, waiting for transfers between devices, body(): lax.ppermute(sent, 'chan', [(d, (d + hop) % ways) for d in range(ways)])  47.9 us
    dot_general x1, matrix products, row_spectrum_pass(): freqs = jnp.einsum('kpnc,pqknj->kqjc', section, second, precision=HIGH)  47.4 us
    dot_general x1, matrix products, row_spectrum_pass(): rows = jnp.einsum('kpnc,pqjk->qjnc', section, last, precision=HIGH)  40.1 us
    dot_general x2, matrix products, partial(): lax.dot_general(part[0], table_real, wide, precision=HIGH)  38.2 us
    psum x1, blocking collectives, body(): norm_now, curvature, cross, square = lax.psum(moments, ('chan', 'facet'))  38.2 us
    dot_general x2, matrix products, partial(): lax.dot_general(part[1], table_imag, wide, precision=HIGH)  36.5 us
  transfers between devices with their start and end apart: 14, of which 4 were waited for; matrix products, arithmetic and copies ran while one was open for 25% of the time, Pallas kernels for 0%

profile of v1, /device:TPU:0, one launch (start us, length us, event | category | flops | bytes accessed | tf_op | source)
XLA Modules:
  0.0 651.9 jit_solution(10965610321289318407)
XLA Ops:
  0.6 3.0 collective-permute-start.1
  3.7 8.5 %copy.41 = f32[1,512,2048]{2,0,1:T(1,128)} copy(f32[1,512,2048]{2,1,0:T(8,128)} %param.8) | data formatting | bytes 8388608 | tf_op args[2]
  12.2 6.1 all-to-all-start
  20.1 7.2 %multiply_add_fusion = (f32[32,64,1024]{2,1,0:T(8,128)}, f32[32,64,1024]{2,1,0:T(8,128)}) fusion(f32[64,1024]{1,0:T(8,128)S(1)} %get-tuple-element.40, f32[32,1024]{1,0:T(8,128)S(1)} %get-tuple-element.38, f32[64,1024]{1,0:T(8,128)S(1)} %get-tuple-element.39, f32[32,1024]{1,0:T(8,128)S(1)} %get-tuple-element.37), kind=kLoop, calls=%fused_computation.25 | loop fusion | flops 12582912 | bytes 17563648 | tf_op jit(solution)/shard_map/add | solution.py:35
  27.5 17.7 %copy.89 = f32[64,64,1024]{2,0,1:T(8,128)} copy(f32[64,64,1024]{2,1,0:T(8,128)} %bitcast.123) | data formatting | bytes 33554432 | tf_op jit(solution)/shard_map/reshape;squeeze | solution.py:54
  45.5 8.3 %fusion.42 = (f32[1,64,64,64]{2,3,0,1:T(8,128)S(1)}, f32[1,64,64,64]{2,3,0,1:T(8,128)S(1)}, f32[1,64,64,64]{2,3,0,1:T(8,128)S(1)}, f32[1,64,64,64]{2,3,0,1:T(8,128)S(1)}, f32[1,64,64,64]{2,3,0,1:T(8,128)S(1)}) fusion(s32[64,64]{0,1:T(8,128)S(1)} %broadcast_multiply_fusion.1, s32[64,64]{1,0:T(8,128)S(1)} %copy.30), kind=kLoop, calls=%fused_computation.75 | loop fusion | flops 4456448 | bytes 5275648 | tf_op jit(solution)/shard_map/sin | solution.py:15
  53.8 40.8 %collective-permute-done.1 = f32[512,2048]{1,0:T(8,128)} collective-permute-done((f32[512,2048]{1,0:T(8,128)}, f32[512,2048]{1,0:T(8,128)}, u32[]{:S(2)}, u32[]{:S(2)}) %collective-permute-start.1) | collective-permute-done | bytes 4194336 | tf_op jit(solution)/shard_map/ppermute | solution.py:24
  94.8 6.8 %fusion.24 = (f32[1,2,64,64,64]{3,4,1,2,0:T(8,128)}, f32[1,2,64,64,64]{3,4,1,2,0:T(8,128)}, f32[1,2,64,64,64]{3,4,1,2,0:T(8,128)}, f32[1,2,64,64,64]{3,4,1,2,0:T(8,128)}) fusion(f32[1,64,64,64]{2,3,0,1:T(8,128)S(1)} %get-tuple-element.32, f32[1,64,64,64]{2,3,0,1:T(8,128)S(1)} %get-tuple-element.28, f32[1,64,64,64]{2,3,0,1:T(8,128)S(1)} %get-tuple-element.29, ...), kind=kLoop, calls=%fused_computation.36 | loop fusion | flops 2097152 | bytes 13631488 | tf_op jit(solution)/shard_map/stack | solution.py:40
  101.5 5.0 constant_dynamic-update-slice_fusion.1
  106.6 18.2 %fusion.18 = f32[1024,1024]{1,0:T(8,128)} fusion(f32[2048,1024]{1,0:T(8,128)S(1)} %bitcast.132, f32[512,2048]{1,0:T(8,128)} %collective-permute-done, f32[512,2048]{1,0:T(8,128)S(1)} %bitcast.119), kind=kOutput, calls=%fused_computation.28 | convolution fusion | flops 12886999040 | bytes 20971520 | tf_op jit(solution)/shard_map/dot_general | solution.py:85
  124.8 18.0 %fusion.17 = f32[1024,1024]{1,0:T(8,128)} fusion(f32[2048,1024]{1,0:T(8,128)S(1)} %bitcast.140, f32[512,2048]{1,0:T(8,128)} %collective-permute-done, f32[512,2048]{1,0:T(8,128)S(1)} %bitcast.120), kind=kOutput, calls=%fused_computation.27 | convolution fusion | flops 12886999040 | bytes 20971520 | tf_op jit(solution)/shard_map/dot_general | solution.py:85
  142.8 4.1 copy.65
  146.9 6.4 fusion.35
  153.3 5.1 fusion.84
  158.4 4.9 constant_dynamic-update-slice_fusion
  163.3 17.8 %fusion.82 = f32[1024,1024]{1,0:T(8,128)} fusion(f32[1024,2048]{1,0:T(8,128)} %constant_dynamic-update-slice_fusion, f32[2048,1024]{1,0:T(8,128)S(1)} %bitcast.135), kind=kOutput, calls=%fused_computation.160 | convolution fusion | flops 12884901888 | bytes 20971520 | tf_op jit(solution)/shard_map/dot_general | solution.py:85
  181.0 18.1 %fusion.83 = f32[1024,1024]{1,0:T(8,128)} fusion(f32[1024,2048]{1,0:T(8,128)} %constant_dynamic-update-slice_fusion, f32[2048,1024]{1,0:T(8,128)S(1)} %bitcast.143), kind=kOutput, calls=%fused_computation.161 | convolution fusion | flops 12884901888 | bytes 20971520 | tf_op jit(solution)/shard_map/dot_general | solution.py:85
  199.1 3.3 pad_maximum_fusion.2
  202.4 8.1 %copy.32 = f32[1,32,64,1024]{3,1,0,2:T(8,128)} copy(f32[1,32,64,1024]{3,2,1,0:T(8,128)S(1)} %bitcast.121) | data formatting | bytes 16777216 | tf_op jit(solution)/shard_map/stack | solution.py:82
  210.6 3.8 pad_maximum_fusion.3
  214.3 8.1 %copy.33 = f32[1,32,64,1024]{3,1,0,2:T(8,128)} copy(f32[1,32,64,1024]{3,2,1,0:T(8,128)S(1)} %bitcast.122) | data formatting | bytes 16777216 | tf_op jit(solution)/shard_map/stack | solution.py:82
  222.4 27.8 %convolution_bitcast_fusion = f32[64,2,64,1024,1]{3,0,2,1,4:T(8,128)} fusion(f32[1,32,64,1024]{3,1,0,2:T(8,128)} %copy.33, f32[1,32,64,1024]{3,1,0,2:T(8,128)} %copy.32, f32[1,2,32,64]{3,2,0,1:T(8,128)S(1)} %get-tuple-element.34, f32[1,2,32,64]{3,2,0,1:T(8,128)S(1)} %get-tuple-element.35), kind=kOutput, calls=%fused_computation.9 | convolution fusion | flops 3225427968 | bytes 50364416 | tf_op jit(solution)/shard_map/pjnc,pqjk->kqnc/dot_general | solution.py:47
  250.2 47.4 %fusion.6 = f32[64,2,64,1024,1]{3,2,0,1,4:T(8,128)} fusion(f32[64,2,64,1024,1]{3,0,2,1,4:T(8,128)} %convolution_bitcast_fusion, f32[1,2,64,64,64]{3,4,1,2,0:T(8,128)} %get-tuple-element.23, f32[1,2,64,64,64]{3,4,1,2,0:T(8,128)} %get-tuple-element.24), kind=kOutput, calls=%fused_computation.7 | convolution fusion | flops 6443499520 | bytes 71303168 | tf_op jit(solution)/shard_map/kpnc,pqknj->kqjc/dot_general | solution.py:53
  297.7 32.3 %fusion.10 = f32[64,2,64,1024]{3,2,1,0:T(8,128)} fusion(f32[1,2,64,64,64]{3,4,1,2,0:T(8,128)} %get-tuple-element.25, f32[1,2,64,64,64]{3,4,1,2,0:T(8,128)} %get-tuple-element.22, f32[64,2,64,1024,1]{3,2,0,1,4:T(8,128)} %fusion.6, f32[64,64,1024]{2,1,0:T(8,128)} %bitcast.114), kind=kOutput, calls=%fused_computation.14 | convolution fusion | flops 6451888128 | bytes 88080384 | tf_op jit(solution)/shard_map/kpjc,pqknj->kqnc/dot_general | solution.py:57
  329.9 40.1 %fusion.19 = f32[2,32,64,1024]{3,1,2,0:T(8,128)S(1)} fusion(f32[64,2,64,1024]{3,2,1,0:T(8,128)} %fusion.10, f32[1,2,32,64]{3,2,1,0:T(8,128)S(1)} %get-tuple-element.36, f32[1,2,32,64]{3,2,1,0:T(8,128)S(1)} %get-tuple-element.33), kind=kOutput, calls=%fused_computation.29 | convolution fusion | flops 3221233664 | bytes 50364416 | tf_op jit(solution)/shard_map/kpnc,pqjk->qjnc/dot_general | solution.py:59
  370.1 19.4 %copy.40 = f32[2,32,64,1024]{3,2,1,0:T(8,128)} copy(f32[2,32,64,1024]{3,1,2,0:T(8,128)S(1)} %fusion.19) | data formatting | bytes 33554432 | tf_op jit(solution)/shard_map/kpnc,pqjk->qjnc/dot_general | solution.py:59
  389.4 18.1 %fusion.27 = f32[1024,2048]{1,0:T(8,128)} fusion(f32[2048,1024]{1,0:T(8,128)} %bitcast.136, f32[2,2048,1024]{2,1,0:T(8,128)} %bitcast.124), kind=kOutput, calls=%fused_computation.41 | convolution fusion | flops 12884901888 | bytes 20971520 | tf_op jit(solution)/shard_map/dot_general | solution.py:96
  407.6 17.9 %fusion.38 = f32[1024,2048]{1,0:T(8,128)S(1)} fusion(f32[1024,2048]{1,0:T(8,128)} %fusion.27, f32[2048,1024]{1,0:T(8,128)} %bitcast.128, f32[2,2048,1024]{2,1,0:T(8,128)} %bitcast.125), kind=kOutput, calls=%fused_computation.67 | convolution fusion | flops 12886999040 | bytes 29360128 | tf_op jit(solution)/shard_map/dot_general | solution.py:96
  425.5 2.4 slice.77
  430.5 2.8 copy_add_fusion
  434.4 1.7 fusion.80
  436.1 4.8 collective-permute-start.6
  441.4 3.0 collective-permute-start.9
  444.3 18.3 %fusion.33 = f32[1024,2048]{1,0:T(8,128)} fusion(f32[2048,1024]{1,0:T(8,128)} %bitcast.137, f32[2,2048,1024]{2,1,0:T(8,128)} %bitcast.126), kind=kOutput, calls=%fused_computation.50 | convolution fusion | flops 12884901888 | bytes 20971520 | tf_op jit(solution)/shard_map/dot_general | solution.py:96
  462.7 20.2 %fusion.37 = f32[1024,2048]{1,0:T(8,128)} fusion(f32[1024,2048]{1,0:T(8,128)} %fusion.33, f32[2048,1024]{1,0:T(8,128)} %bitcast.129, f32[2,2048,1024]{2,1,0:T(8,128)} %bitcast.127), kind=kOutput, calls=%fused_computation.66 | convolution fusion | flops 12886999040 | bytes 29360128 | tf_op jit(solution)/shard_map/dot_general | solution.py:96
  482.9 4.7 slice.73
  487.6 2.0 copy-done.8
  489.6 2.8 slice_add_fusion
  492.5 1.6 collective-permute-start.5
  494.3 5.3 collective-permute-start.11
  499.7 31.8 %collective-permute-done.9 = f32[1,64,2048]{2,1,0:T(8,128)S(1)} collective-permute-done((f32[1,64,2048]{2,1,0:T(8,128)}, f32[1,64,2048]{2,1,0:T(8,128)S(1)}, u32[]{:S(2)}, u32[]{:S(2)}) %collective-permute-start.9) | collective-permute-done | bytes 524320 | tf_op jit(solution)/shard_map/ppermute | solution.py:128
  531.9 16.0 %collective-permute-done.12 = f32[1,64,2048]{2,1,0:T(8,128)S(1)} collective-permute-done((f32[1,64,2048]{2,1,0:T(8,128)S(1)}, f32[1,64,2048]{2,1,0:T(8,128)S(1)}, u32[]{:S(2)}, u32[]{:S(2)}) %collective-permute-start.12) | collective-permute-done | bytes 524320 | tf_op jit(solution)/shard_map/ppermute | solution.py:128
  548.4 3.3 copy-done.11
  551.6 34.1 %collective-permute-done.5 = f32[512,2048]{1,0:T(8,128)} collective-permute-done((f32[512,2048]{1,0:T(8,128)S(1)}, f32[512,2048]{1,0:T(8,128)}, u32[]{:S(2)}, u32[]{:S(2)}) %collective-permute-start.5) | collective-permute-done | bytes 4194336 | tf_op jit(solution)/shard_map/ppermute | solution.py:24
  585.7 7.7 %multiply_reduce_fusion.3 = (f32[]{:T(128)}, f32[]{:T(128)}, f32[]{:T(128)}, f32[]{:T(128)}, f32[1,512,2048]{2,1,0:T(8,128)}) fusion(f32[1,512,2048]{2,1,0:T(8,128)S(1)} %copy-done.7, f32[1,512,2048]{2,1,0:T(8,128)S(1)} %copy-done.5, f32[1,1024,2048]{2,1,0:T(8,128)} %copy-done.11, s32[]{:T(128)S(6)} %select_n.132, f32[512,2048]{1,0:T(8,128)} %collective-permute-done.5, ...), kind=kLoop, calls=%fused_computation.62 | loop fusion | flops 12582908 | bytes 29360148 | tf_op jit(solution)/shard_map/reduce_sum | solution.py:134
  593.5 2.6 pad_maximum_fusion.14
  596.0 38.2 %psum.7 = f32[4]{0:T(128)S(1)} all-reduce(f32[4]{0:T(128)S(1)} %pad_maximum_fusion.14), channel_id=1, replica_groups=mesh['chan'=8,'facet'=4] {'chan','facet'}, use_global_device_ids=true, to_apply=%region_4.5 | all-reduce | flops 4 | bytes 32 | tf_op jit(solution)/shard_map/psum | solution.py:140
  638.6 12.8 %multiply_add_fusion.1 = (f32[1,512,2048]{2,1,0:T(8,128)}, f32[1,512,2048]{2,1,0:T(8,128)}, f32[1,512,2048]{2,1,0:T(8,128)}) fusion(f32[1,512,2048]{2,1,0:T(8,128)} %param.8, f32[]{:T(128)S(6)} %div.7, f32[1,512,2048]{2,1,0:T(8,128)} %param.7, f32[1,512,2048]{2,1,0:T(8,128)} %get-tuple-element.13, f32[]{:T(128)S(6)} %div.6, f32[1,512,2048]{2,1,0:T(8,128)} %param.6), kind=kLoop, calls=%fused_computation.56 | loop fusion | flops 6291456 | bytes 29360136 | tf_op jit(solution)/shard_map/add | solution.py:145
  (102 shorter events, 8.0 us)
Async XLA Ops:
  0.6 44.7 %copy-start = (f32[8,8]{1,0:T(8,128)S(1)}, f32[8,8]{1,0:T(8,128)}, u32[]{:S(2)}) copy-start(f32[8,8]{1,0:T(8,128)} %param.10) | copy-start | bytes 772
  0.6 93.9 %collective-permute-start.1 = (f32[512,2048]{1,0:T(8,128)}, f32[512,2048]{1,0:T(8,128)}, u32[]{:S(2)}, u32[]{:S(2)}) collective-permute-start(f32[512,2048]{1,0:T(8,128)} %bitcast.117), channel_id=1, source_target_pairs={{0,2},{1,3},{2,0},{3,1},{4,6},{5,7},{6,4},{7,5},{8,10},{9,11},{10,... | collective-permute-start | bytes 12582920 | tf_op jit(solution)/shard_map/ppermute | solution.py:24
  12.2 130.5 %all-to-all-start = ((f32[1,512,2048]{2,0,1:T(1,128)}), f32[1,512,2048]{2,0,1:T(1,128)}, u32[]{:S(2)}, u32[]{:S(2)}) async-start(f32[1,512,2048]{2,0,1:T(1,128)} %copy.41), calls=%async_computation | async-start | bytes 8388608 | tf_op jit(solution)/shard_map/all_to_all | solution.py:115
  18.3 88.2 %collective-permute-start = (f32[512,2048]{1,0:T(8,128)}, f32[512,2048]{1,0:T(8,128)}, u32[]{:S(2)}, u32[]{:S(2)}) collective-permute-start(f32[512,2048]{1,0:T(8,128)} %bitcast.118), channel_id=1, source_target_pairs={{0,1},{1,0},{2,3},{3,2},{4,5},{5,4},{6,7},{7,6},{8,9},{9,8},{10,11... | collective-permute-start | bytes 12582920 | tf_op jit(solution)/shard_map/ppermute | solution.py:24
  27.5 17.8 %copy-start.14 = (s32[8]{0:T(128)S(1)}, s32[8]{0:T(128)}, u32[]{:S(2)}) copy-start(s32[8]{0:T(128)} %param.11) | copy-start | bytes 100
  45.5 61.0 %slice-start = ((s8[8388608]{0:T(1024)(128)(4,1)}), s8[4194304]{0:T(1024)(128)(4,1)S(1)}, s32[]{:S(2)}) async-start(s8[8388608]{0:T(1024)(128)(4,1)} %bitcast.130), calls=%async_computation.1 | async-start | bytes 8388608
  94.6 63.8 %collective-permute-start.2 = (f32[512,2048]{1,0:T(8,128)}, f32[512,2048]{1,0:T(8,128)}, u32[]{:S(2)}, u32[]{:S(2)}) collective-permute-start(f32[512,2048]{1,0:T(8,128)} %collective-permute-done.1), channel_id=1, source_target_pairs={{0,1},{1,0},{2,3},{3,2},{4,5},{5,4},{6,7},{7,6},{8,9},{9,8},{10,11... | collective-permute-start | bytes 12582920 | tf_op jit(solution)/shard_map/ppermute | solution.py:24
  94.8 11.8 %slice-start.1 = ((s8[8388608]{0:T(1024)(128)(4,1)}), s8[4194304]{0:T(1024)(128)(4,1)S(1)}, s32[]{:S(2)}) async-start(s8[8388608]{0:T(1024)(128)(4,1)} %bitcast.130), calls=%async_computation.2 | async-start | bytes 8388608
  101.5 5.0 copy-start.4
  101.5 23.2 %slice-start.4 = ((s8[8388608]{0:T(1024)(128)(4,1)}), s8[4194304]{0:T(1024)(128)(4,1)S(1)}, s32[]{:S(2)}) async-start(s8[8388608]{0:T(1024)(128)(4,1)} %bitcast.138), calls=%async_computation.5 | async-start | bytes 8388608
  106.5 18.2 %slice-start.5 = ((s8[8388608]{0:T(1024)(128)(4,1)}), s8[4194304]{0:T(1024)(128)(4,1)S(1)}, s32[]{:S(2)}) async-start(s8[8388608]{0:T(1024)(128)(4,1)} %bitcast.138), calls=%async_computation.6 | async-start | bytes 8388608
  146.9 11.5 %copy-start.2 = (f32[1,512,2048]{2,1,0:T(8,128)}, f32[1,512,2048]{2,1,0:T(8,128)S(1)}, u32[]{:S(2)}) copy-start(f32[1,512,2048]{2,1,0:T(8,128)S(1)} %copy.65) | copy-start | bytes 12582916
  146.9 16.4 %slice-start.2 = ((s8[8388608]{0:T(1024)(128)(4,1)}), s8[4194304]{0:T(1024)(128)(4,1)S(1)}, s32[]{:S(2)}) async-start(s8[8388608]{0:T(1024)(128)(4,1)} %bitcast.133), calls=%async_computation.3 | async-start | bytes 8388608
  153.3 10.0 %slice-start.3 = ((s8[8388608]{0:T(1024)(128)(4,1)}), s8[4194304]{0:T(1024)(128)(4,1)S(1)}, s32[]{:S(2)}) async-start(s8[8388608]{0:T(1024)(128)(4,1)} %bitcast.133), calls=%async_computation.4 | async-start | bytes 8388608
  158.4 22.6 %slice-start.6 = ((s8[8388608]{0:T(1024)(128)(4,1)}), s8[4194304]{0:T(1024)(128)(4,1)S(1)}, s32[]{:S(2)}) async-start(s8[8388608]{0:T(1024)(128)(4,1)} %bitcast.141), calls=%async_computation.7 | async-start | bytes 8388608
  163.3 17.8 %slice-start.7 = ((s8[8388608]{0:T(1024)(128)(4,1)}), s8[4194304]{0:T(1024)(128)(4,1)S(1)}, s32[]{:S(2)}) async-start(s8[8388608]{0:T(1024)(128)(4,1)} %bitcast.141), calls=%async_computation.8 | async-start | bytes 8388608
  181.0 18.1 %copy-start.10 = (f32[1024,1024]{1,0:T(8,128)S(1)}, f32[1024,1024]{1,0:T(8,128)}, u32[]{:S(2)}) copy-start(f32[1024,1024]{1,0:T(8,128)} %fusion.18) | copy-start | bytes 12582916
  202.4 8.2 %copy-start.9 = (f32[1024,1024]{1,0:T(8,128)S(1)}, f32[1024,1024]{1,0:T(8,128)}, u32[]{:S(2)}) copy-start(f32[1024,1024]{1,0:T(8,128)} %fusion.17) | copy-start | bytes 12582916
  425.5 3.7 copy-start.3
  425.5 5.0 copy-start.6
  427.9 59.7 %collective-permute-start.4 = (f32[512,2048]{1,0:T(8,128)}, f32[512,2048]{1,0:T(8,128)S(1)}, u32[]{:S(2)}, u32[]{:S(2)}) collective-permute-start(f32[512,2048]{1,0:T(8,128)} %slice.77), channel_id=1, source_target_pairs={{0,1},{1,0},{2,3},{3,2},{4,5},{5,4},{6,7},{7,6},{8,9},{9,8},{10,11... | collective-permute-start | bytes 12582920 | tf_op jit(solution)/shard_map/ppermute | solution.py:24
  436.1 56.4 %collective-permute-start.6 = (f32[1,64,2048]{2,1,0:T(8,128)}, f32[1,64,2048]{2,1,0:T(8,128)S(1)}, u32[]{:S(2)}, u32[]{:S(2)}) collective-permute-start(f32[1,64,2048]{2,1,0:T(8,128)} %get-tuple-element.21), channel_id=1, source_target_pairs={{0,28},{4,0},{8,4},{12,8},{16,12},{20,16},{24,20},{28,24},{1,29},{... | collective-permute-start | bytes 1572872 | tf_op jit(solution)/shard_map/ppermute | solution.py:128
  440.9 53.2 %collective-permute-start.7 = (f32[1,64,2048]{2,1,0:T(8,128)}, f32[1,64,2048]{2,1,0:T(8,128)S(1)}, u32[]{:S(2)}, u32[]{:S(2)}) collective-permute-start(f32[1,64,2048]{2,1,0:T(8,128)} %get-tuple-element.20), channel_id=1, source_target_pairs={{0,24},{4,28},{8,0},{12,4},{16,8},{20,12},{24,16},{28,20},{1,25},{... | collective-permute-start | bytes 1572872 | tf_op jit(solution)/shard_map/ppermute | solution.py:128
  441.4 52.9 %collective-permute-start.8 = (f32[1,64,2048]{2,1,0:T(8,128)}, f32[1,64,2048]{2,1,0:T(8,128)S(1)}, u32[]{:S(2)}, u32[]{:S(2)}) collective-permute-start(f32[1,64,2048]{2,1,0:T(8,128)} %get-tuple-element.19), channel_id=1, source_target_pairs={{0,20},{4,24},{8,28},{12,0},{16,4},{20,8},{24,12},{28,16},{1,21},{... | collective-permute-start | bytes 1572872 | tf_op jit(solution)/shard_map/ppermute | solution.py:128
  441.4 90.1 %collective-permute-start.9 = (f32[1,64,2048]{2,1,0:T(8,128)}, f32[1,64,2048]{2,1,0:T(8,128)S(1)}, u32[]{:S(2)}, u32[]{:S(2)}) collective-permute-start(f32[1,64,2048]{2,1,0:T(8,128)} %get-tuple-element.18), channel_id=1, source_target_pairs={{0,16},{4,20},{8,24},{12,28},{16,0},{20,4},{24,8},{28,12},{1,17},{... | collective-permute-start | bytes 1572872 | tf_op jit(solution)/shard_map/ppermute | solution.py:128
  487.6 6.5 %copy-start.13 = (f32[1,64,2048]{2,1,0:T(8,128)S(1)}, f32[1,64,2048]{2,1,0:T(8,128)}, u32[]{:S(2)}) copy-start(f32[1,64,2048]{2,1,0:T(8,128)} %get-tuple-element.17) | copy-start | bytes 1572868
  487.6 6.7 %copy-start.12 = (f32[1,64,2048]{2,1,0:T(8,128)S(1)}, f32[1,64,2048]{2,1,0:T(8,128)}, u32[]{:S(2)}) copy-start(f32[1,64,2048]{2,1,0:T(8,128)} %get-tuple-element.16) | copy-start | bytes 1572868
  487.6 2.0 copy-start.8
  489.6 62.0 %collective-permute-start.3 = (f32[512,2048]{1,0:T(8,128)}, f32[512,2048]{1,0:T(8,128)}, u32[]{:S(2)}, u32[]{:S(2)}) collective-permute-start(f32[512,2048]{1,0:T(8,128)} %slice.73), channel_id=1, source_target_pairs={{0,1},{1,0},{2,3},{3,2},{4,5},{5,4},{6,7},{7,6},{8,9},{9,8},{10,11... | collective-permute-start | bytes 12582920 | tf_op jit(solution)/shard_map/ppermute | solution.py:24
  489.6 96.0 %slice-start.8 = ((s8[8388608]{0:T(1024)(128)(4,1)}), s8[4194304]{0:T(1024)(128)(4,1)S(1)}, s32[]{:S(2)}) async-start(s8[8388608]{0:T(1024)(128)(4,1)} %bitcast.144), calls=%async_computation.9 | async-start | bytes 8388608
  492.5 93.2 %copy-start.5 = (f32[1,512,2048]{2,1,0:T(8,128)S(1)}, f32[1,512,2048]{2,1,0:T(8,128)}, u32[]{:S(2)}) copy-start(f32[1,512,2048]{2,1,0:T(8,128)} %param.8) | copy-start | bytes 12582916
  492.5 93.2 %copy-start.7 = (f32[1,512,2048]{2,1,0:T(8,128)S(1)}, f32[1,512,2048]{2,1,0:T(8,128)}, u32[]{:S(2)}) copy-start(f32[1,512,2048]{2,1,0:T(8,128)} %param.7) | copy-start | bytes 12582916
  492.5 93.2 %collective-permute-start.5 = (f32[512,2048]{1,0:T(8,128)S(1)}, f32[512,2048]{1,0:T(8,128)}, u32[]{:S(2)}, u32[]{:S(2)}) collective-permute-start(f32[512,2048]{1,0:T(8,128)S(1)} %slice_add_fusion), channel_id=1, source_target_pairs={{0,2},{1,3},{2,0},{3,1},{4,6},{5,7},{6,4},{7,5},{8,10},{9,11},{10,... | collective-permute-start | bytes 12582920 | tf_op jit(solution)/shard_map/ppermute | solution.py:24
  494.2 37.6 %collective-permute-start.10 = (f32[1,64,2048]{2,1,0:T(8,128)S(1)}, f32[1,64,2048]{2,1,0:T(8,128)S(1)}, u32[]{:S(2)}, u32[]{:S(2)}) collective-permute-start(f32[1,64,2048]{2,1,0:T(8,128)S(1)} %copy-done.13), channel_id=1, source_target_pairs={{0,12},{4,16},{8,20},{12,24},{16,28},{20,0},{24,4},{28,8},{1,13},{... | collective-permute-start | bytes 1572872 | tf_op jit(solution)/shard_map/ppermute | solution.py:128
  494.3 91.4 %slice-start.9 = ((s8[8388608]{0:T(1024)(128)(4,1)}), s8[4194304]{0:T(1024)(128)(4,1)S(1)}, s32[]{:S(2)}) async-start(s8[8388608]{0:T(1024)(128)(4,1)} %bitcast.144), calls=%async_computation.10 | async-start | bytes 8388608
  494.3 37.6 %collective-permute-start.11 = (f32[1,64,2048]{2,1,0:T(8,128)S(1)}, f32[1,64,2048]{2,1,0:T(8,128)S(1)}, u32[]{:S(2)}, u32[]{:S(2)}) collective-permute-start(f32[1,64,2048]{2,1,0:T(8,128)S(1)} %copy-done.12), channel_id=1, source_target_pairs={{0,8},{4,12},{8,16},{12,20},{16,24},{20,28},{24,0},{28,4},{1,9},{5... | collective-permute-start | bytes 1572872 | tf_op jit(solution)/shard_map/ppermute | solution.py:128
  531.5 16.4 %collective-permute-start.12 = (f32[1,64,2048]{2,1,0:T(8,128)S(1)}, f32[1,64,2048]{2,1,0:T(8,128)S(1)}, u32[]{:S(2)}, u32[]{:S(2)}) collective-permute-start(f32[1,64,2048]{2,1,0:T(8,128)S(1)} %get-tuple-element.15), channel_id=1, source_target_pairs={{0,4},{4,8},{8,12},{12,16},{16,20},{20,24},{24,28},{28,0},{1,5},{5... | collective-permute-start | bytes 1572872 | tf_op jit(solution)/shard_map/ppermute | solution.py:128
  548.3 3.3 copy-start.11
  638.6 12.8 %copy-start.1 = (f32[8,8]{1,0:T(8,128)S(1)}, f32[8,8]{1,0:T(8,128)}, u32[]{:S(2)}) copy-start(f32[8,8]{1,0:T(8,128)} %param.10) | copy-start | bytes 772
